TPU v7x, 32 devices: a whole 2x2x4 slice. The times are simulated.
32 devices in a mesh: vec: 4 (over x, core), lat: 8 (over z, y).
Axes of the slice: x: 2, y: 2, z: 4, core: 2. Of those that a mesh axis runs over, the one named last changes fastest.
Arguments:
- perturbation: float32 [32, 3, 64, 2048], P('vec', None, 'lat'), may hold values from -6 to 6
- wind_coriolis: float32 [4, 3, 64, 2048], P(None, None, 'lat', 'vec'), may hold values from -4 to 4
- depth_field: float32 [4, 64, 2048], P(None, 'lat', 'vec'), may hold values from 0.5 to 2
Outputs:
- evolved: float32 [32, 3, 64, 2048], P('vec', None, 'lat')
All inputs are finite; a program needn't handle non-finite values.
Results may differ from a plain program's by a relative error of at most 0.00002.
Values sent between devices are 32-bit elements; how exact they have to be, the bound alone decides.
A program may use at most 64 MiB of HBM per device.

v0:
```python
import functools

import jax
import jax.numpy as jnp
from jax import lax
from jax.experimental import pallas as pl
from jax.experimental.pallas import tpu as pltpu
from jax.sharding import PartitionSpec as P

MESH = pl.DeviceIdType.MESH
LANES = 128
time_step = 0.2
viscosity = 0.05
side_weight = time_step * viscosity
half_step = 0.5 * time_step


def sweep(load, store, coefficient, sides, tiles, keep):
    lane = lax.broadcasted_iota(jnp.int32, (8, LANES), 1)
    row = lax.broadcasted_iota(jnp.int32, (8, LANES), 0)
    first_lane, last_lane = lane == 0, lane == LANES - 1
    first_row, last_row = row == 0, row == 7
    known = {}

    def tile(side, field, t):
        key = (side, field, t)
        if key not in known:
            value = load(side, field, t % tiles)
            known[key] = (value, pltpu.roll(value, LANES - 1, 1), pltpu.roll(value, 1, 1))
        return known[key]

    for t in range(tiles):
        east, west, rise, fall, here = {}, {}, {}, {}, {}
        for field in range(3):
            turned = []
            for side in range(2):
                value = tile(side, field, t)[0] if side in sides else load(side, field, t)
                turned.append((pltpu.roll(value, 7, 0), pltpu.roll(value, 1, 0)))
            for side in sides:
                before, now, after = (tile(side, field, t + k) for k in (-1, 0, 1))
                here[side, field] = now[0]
                east[side, field] = jnp.where(last_lane, after[1], now[1])
                west[side, field] = jnp.where(first_lane, before[2], now[2])
                rise[side, field] = jnp.where(last_row, turned[1 - side][0], turned[side][0])
                fall[side, field] = jnp.where(first_row, turned[1 - side][1], turned[side][1])
        for side in sides:
            to_east, to_west, to_rise, to_fall, d, c = (coefficient(side, q, t) for q in range(6))
            new = [
                (1.0 - 4.0 * side_weight) * here[side, f]
                + (to_east * east[side, f] + to_west * west[side, f])
                + (to_rise * rise[side, f] + to_fall * fall[side, f])
                for f in range(3)
            ]
            new[0] -= c * ((east[side, 1] - west[side, 1]) + (rise[side, 2] - fall[side, 2]))
            new[1] += d * here[side, 2] - half_step * (east[side, 0] - west[side, 0])
            new[2] -= d * here[side, 1] + half_step * (rise[side, 0] - fall[side, 0])
            for f in range(3):
                store(side, f, t, new[f] if side == 0 else jnp.where(keep, new[f], 0.0))


def kernel(
    nv, nl, x_hbm, wind, depth, out,
    x, halo, transit, ping, pong, own, ring, table,
    x_sem, own_sem,
    gs, gr, cs, cr, fs, fr, hs, hr, ts, tr,
):
    count, _, rows, width = x_hbm.shape
    steps, part = wind.shape[0], wind.shape[3]
    tiles, reach = width // LANES, steps
    v, l = lax.axis_index("vec"), lax.axis_index("lat")
    has = (l > 0, l < nl - 1)
    other = (l - 1, l + 1)
    far = (l - 2, l + 2)
    reaches = (l > 1, l < nl - 2)
    pairs = nl // 2
    odd = lax.rem(l, 2)
    place = l // 2

    def share(number, wanted):
        return jnp.where(wanted, number * count // pairs, 0) if nl % 2 == 0 else jnp.int32(0)

    relayed = (
        share(place, (odd == 0) & reaches[0]),
        share(pairs - 1 - place, (odd == 1) & reaches[1]),
    )
    relaying = (
        share(place, (odd == 1) & reaches[0]),
        share(pairs - 1 - place, (odd == 0) & reaches[1]),
    )
    peers = [lax.rem(v + k, nv) for k in range(1, nv)]
    edge = (lambda n: pl.ds(0, n), lambda n: pl.ds(rows - n, n))

    local = [
        pltpu.make_async_copy(x_hbm, x, x_sem.at[0]),
        pltpu.make_async_copy(wind, own.at[v, :, pl.ds(0, 3)], own_sem.at[0]),
        pltpu.make_async_copy(depth, own.at[v, :, 3], own_sem.at[1]),
    ]
    for copy in local:
        copy.start()

    barrier = pltpu.get_barrier_semaphore()
    for peer in peers:
        pl.semaphore_signal(barrier, inc=1, device_id={"vec": peer}, device_id_type=MESH)
    for side in range(2):
        @pl.when(has[side])
        def _(side=side):
            pl.semaphore_signal(barrier, inc=1, device_id={"lat": other[side]}, device_id_type=MESH)
        @pl.when(reaches[side])
        def _(side=side):
            pl.semaphore_signal(barrier, inc=1, device_id={"lat": far[side]}, device_id_type=MESH)
    pl.semaphore_wait(barrier, nv - 1 + sum(flag.astype(jnp.int32) for flag in has + reaches))

    def remote(src, dst, send, recv, target):
        return pltpu.make_async_remote_copy(
            src_ref=src, dst_ref=dst, send_sem=send, recv_sem=recv,
            device_id=target, device_id_type=MESH,
        )

    def edges(side):
        made = []
        for s in range(steps - 1):
            at = edge[side](reach - 1 - s)
            made.append(remote(
                wind.at[s, :, at, :], ring.at[v, s, pl.ds(0, 3), at, :],
                cs.at[side, s, 0], cr.at[side, s, 0], {"lat": other[side]}))
            made.append(remote(
                depth.at[s, at, :], ring.at[v, s, 3, at, :],
                cs.at[side, s, 1], cr.at[side, s, 1], {"lat": other[side]}))
        return made

    def state(side, k):
        at = edge[side](reach)
        return remote(
            x_hbm.at[k, :, at, :], halo.at[k, :, at, :],
            hs.at[side, k], hr.at[side, k], {"lat": other[side]})

    def detour(side, k):
        at = edge[side](reach)
        return remote(
            x_hbm.at[k, :, at, :], transit.at[k, :, at, :],
            hs.at[side, k], tr.at[k], {"lat": other[1 - side]})

    def onward(side, k):
        at = edge[side](reach)
        return remote(
            transit.at[k, :, at, :], halo.at[k, :, at, :],
            ts.at[k], hr.at[side, k], {"lat": far[side]})

    def spread(n, peer):
        return [
            remote(wind, own.at[v, :, pl.ds(0, 3)], gs.at[n, 0], gr.at[n, 0], {"vec": peer}),
            remote(depth, own.at[v, :, 3], gs.at[n, 1], gr.at[n, 1], {"vec": peer}),
        ]

    def passed(side, n, peer):
        made = []
        for s in range(steps - 1):
            at = edge[side](reach - 1 - s)
            made.append(remote(
                ring.at[v, s, :, at, :], ring.at[v, s, :, at, :],
                fs.at[side, n, s], fr.at[side, n, s], {"vec": peer}))
        return made

    for side in range(2):
        @pl.when(has[side])
        def _(side=side):
            for copy in edges(side):
                copy.start()

    @pl.loop(0, count)
    def _(k):
        for side in range(2):
            @pl.when(k < relayed[side])
            def _(side=side):
                detour(side, k).start()

    @pl.loop(0, count)
    def _(k):
        for side in range(2):
            @pl.when(has[side] & (k >= relayed[side]))
            def _(side=side):
                state(side, k).start()

    for n, peer in enumerate(peers):
        for copy in spread(n, peer):
            copy.start()

    for side in range(2):
        @pl.when(jnp.logical_not(has[1 - side]))
        def _(side=side):
            halo[:, :, edge[side](reach), :] = jnp.zeros((count, 3, reach, width), jnp.float32)

    for side in range(2):
        @pl.when(has[1 - side])
        def _(side=side):
            for copy in edges(side):
                copy.wait_recv()
            for n, peer in enumerate(peers):
                for copy in passed(side, n, peer):
                    copy.start()

    @pl.loop(0, count)
    def _(k):
        for side in range(2):
            @pl.when(k < relaying[side])
            def _(side=side):
                detour(side, k).wait_recv()
                onward(side, k).start()
    for copy in local:
        copy.wait()
    for n, peer in enumerate(peers):
        for copy in spread(n, peer):
            copy.wait_recv()
    for side in range(2):
        @pl.when(has[1 - side])
        def _(side=side):
            for n, peer in enumerate(peers):
                for copy in passed(side, n, peer):
                    copy.wait_recv()

    for side in range(2):
        @pl.loop(0, steps - side)
        def _(s, side=side):
            for t in range(tiles):
                block, offset = divmod(t * LANES, part)
                given = (own, ring)[side]
                a, b, d, c = (given[block, s, q, :, pl.ds(offset, LANES)] for q in range(4))
                a, b = half_step * a, half_step * b
                values = (side_weight - a, side_weight + a, side_weight - b, side_weight + b, time_step * d, half_step * c)
                for q, value in enumerate(values):
                    table[side, s, q, :, pl.ds(t * LANES, LANES)] = value

    row = lax.broadcasted_iota(jnp.int32, (8, LANES), 0)

    @pl.loop(0, count)
    def _(k):
        for side in range(2):
            @pl.when(has[1 - side])
            def _(side=side):
                state(side, k).wait_recv()

        def span(t):
            return pl.ds(t * LANES, LANES)

        def first(side, f, t):
            return (x, halo)[side][k, f, :, span(t)]

        def reader(ref):
            return lambda side, f, t: ref[side, f, :, span(t)]

        def writer(ref):
            def put(side, f, t, value):
                ref[side, f, :, span(t)] = value
            return put

        def last(side, f, t, value):
            out[k, f, :, span(t)] = value

        for s in range(steps):
            def coefficient(side, channel, t, s=s):
                return table[side, s, channel, :, span(t)]

            final = s == steps - 1
            good = reach - 1 - s
            keep = ((row < good) & has[1]) | ((row >= rows - good) & has[0])
            sweep(
                first if s == 0 else reader((ping, pong)[(s - 1) % 2]),
                last if final else writer((ping, pong)[s % 2]),
                coefficient, (0,) if final else (0, 1), tiles, keep)

    for side in range(2):
        @pl.when(has[side])
        def _(side=side):
            for copy in edges(side):
                copy.wait_send()
        @pl.when(has[1 - side])
        def _(side=side):
            for n, peer in enumerate(peers):
                for copy in passed(side, n, peer):
                    copy.wait_send()
    for n, peer in enumerate(peers):
        for copy in spread(n, peer):
            copy.wait_send()

    @pl.loop(0, count)
    def _(k):
        for side in range(2):
            @pl.when(has[side])
            def _(side=side):
                state(side, k).wait_send()
            @pl.when(k < relaying[side])
            def _(side=side):
                onward(side, k).wait_send()


def solution(mesh):
    nv, nl = mesh.shape["vec"], mesh.shape["lat"]

    def shards(perturbation, wind_coriolis, depth_field):
        count, _, rows, width = perturbation.shape
        steps, part = wind_coriolis.shape[0], wind_coriolis.shape[3]
        dma = pltpu.SemaphoreType.DMA
        f32 = jnp.float32
        return pl.pallas_call(
            functools.partial(kernel, nv, nl),
            out_shape=jax.ShapeDtypeStruct(perturbation.shape, f32),
            in_specs=[pl.BlockSpec(memory_space=pltpu.HBM)] * 3,
            out_specs=pl.BlockSpec(memory_space=pltpu.VMEM),
            scratch_shapes=[
                pltpu.VMEM((count, 3, rows, width), f32),
                pltpu.VMEM((count, 3, rows, width), f32),
                pltpu.VMEM((count, 3, rows, width), f32),
                pltpu.VMEM((2, 3, rows, width), f32),
                pltpu.VMEM((2, 3, rows, width), f32),
                pltpu.VMEM((nv, steps, 4, rows, part), f32),
                pltpu.VMEM((nv, steps - 1, 4, rows, part), f32),
                pltpu.VMEM((2, steps, 6, rows, width), f32),
                dma((1,)), dma((2,)),
                dma((nv - 1, 2)), dma((nv - 1, 2)),
                dma((2, steps - 1, 2)), dma((2, steps - 1, 2)),
                dma((2, nv - 1, steps - 1)), dma((2, nv - 1, steps - 1)),
                dma((2, count)), dma((2, count)), dma((count,)), dma((count,)),
            ],
            compiler_params=pltpu.CompilerParams(
                collective_id=0, has_side_effects=True, vmem_limit_bytes=40 * 1024 * 1024
            ),
        )(*(pltpu.with_memory_space_constraint(a, pltpu.HBM) for a in (perturbation, wind_coriolis, depth_field)))

    placed = (P("vec", None, "lat", None), P(None, None, "lat", "vec"), P(None, "lat", "vec"))
    return jax.shard_map(
        shards, mesh=mesh, in_specs=placed, out_specs=P("vec", None, "lat", None), check_vma=False
    )
```

profile of v0, /device:TPU:16, one launch (start us, length us, event | category | flops | bytes accessed | tf_op | source)
XLA Modules:
  0.0 39.3 jit_solution(15222114259940555551)
XLA Ops:
  0.0 38.1 %shard_map.37 = f32[8,3,8,2048]{3,2,1,0:T(8,128)S(1)} custom-call(f32[8,3,8,2048]{3,2,1,0:T(8,128)} %x_hbm.1, f32[4,3,8,512]{3,2,1,0:T(8,128)} %wind.1, f32[4,8,512]{2,1,0:T(8,128)} %depth.1), custom_call_target="tpu_custom_call" | custom-call | tf_op jit(solution)/shard_map/pallas_call | solution.py:304
  38.1 1.1 %copy.5 = f32[8,3,8,2048]{3,2,1,0:T(8,128)} copy(f32[8,3,8,2048]{3,2,1,0:T(8,128)S(1)} %shard_map.37) | data formatting | bytes 3145728
where the time goes:
time: 40 us; the launch traced here: 39.3 us
  Pallas kernels  38.1 us (95%)
  local copies, waits for them, and re-layouts  1.15 us (3%)
    pallas_call x1, Pallas kernels, shards(): pl.pallas_call(functools.partial(kernel, nv, nl), out_shape=jax.ShapeDtyp...  38.1 us
    unnamed x1, local copies, waits for them, and re-layouts  1.15 us

commit v1 on v0

v1 whole, which is shorter than its diff:
```python
import functools

import jax
import jax.numpy as jnp
from jax import lax
from jax.experimental import pallas as pl
from jax.experimental.pallas import tpu as pltpu
from jax.sharding import PartitionSpec as P

MESH = pl.DeviceIdType.MESH
LANES = 128
LEAD = 3
time_step = 0.2
viscosity = 0.05
side_weight = time_step * viscosity
half_step = 0.5 * time_step


def sweep(load, store, halo, coefficient, tiles):
    lane = lax.broadcasted_iota(jnp.int32, (8, LANES), 1)
    row = lax.broadcasted_iota(jnp.int32, (8, LANES), 0)
    first_lane, last_lane = lane == 0, lane == LANES - 1
    first_row, last_row = row == 0, row == 7
    known = {}

    def tile(field, t):
        key = (field, t % tiles)
        if key not in known:
            value = load(field, t % tiles)
            known[key] = (value, pltpu.roll(value, LANES - 1, 1), pltpu.roll(value, 1, 1))
        return known[key]

    for t in range(tiles):
        east, west, rise, fall, here = {}, {}, {}, {}, {}
        for f in range(3):
            before, now, after = (tile(f, t + k) for k in (-1, 0, 1))
            here[f] = now[0]
            east[f] = jnp.where(last_lane, after[1], now[1])
            west[f] = jnp.where(first_lane, before[2], now[2])
            rise[f] = jnp.where(last_row, halo(1, f, t), pltpu.roll(now[0], 7, 0))
            fall[f] = jnp.where(first_row, halo(0, f, t), pltpu.roll(now[0], 1, 0))
        to_east, to_west, to_rise, to_fall, d, c = (coefficient(q, t) for q in range(6))
        new = [
            (1.0 - 4.0 * side_weight) * here[f]
            + (to_east * east[f] + to_west * west[f])
            + (to_rise * rise[f] + to_fall * fall[f])
            for f in range(3)
        ]
        new[0] -= c * ((east[1] - west[1]) + (rise[2] - fall[2]))
        new[1] += d * here[2] - half_step * (east[0] - west[0])
        new[2] -= d * here[1] + half_step * (rise[0] - fall[0])
        for f in range(3):
            store(f, t, new[f])


def kernel(
    nv, nl, x_hbm, wind, depth, out,
    ping, pong, leaving, halo, transit, own, table,
    x_sem, own_sem,
    gs, gr, hs, hr, ts, tr,
):
    count, _, rows, width = x_hbm.shape
    steps, part = wind.shape[0], wind.shape[3]
    tiles = width // LANES
    v, l = lax.axis_index("vec"), lax.axis_index("lat")
    has = (l > 0, l < nl - 1)
    other = (l - 1, l + 1)
    far = (l - 2, l + 2)
    reaches = (l > 1, l < nl - 2)
    pairs = nl // 2
    odd = lax.rem(l, 2)
    place = l // 2

    def share(number, wanted):
        return jnp.where(wanted, number * count // pairs, 0) if nl % 2 == 0 else jnp.int32(0)

    relayed = (
        share(place, (odd == 0) & reaches[0]),
        share(pairs - 1 - place, (odd == 1) & reaches[1]),
    )
    relaying = (
        share(place, (odd == 1) & reaches[0]),
        share(pairs - 1 - place, (odd == 0) & reaches[1]),
    )

    def turn(number, s, k):
        if s == steps - 1:
            return k < number
        return lax.rem(k * (count - number), count) >= count - number

    peers = [lax.rem(v + k, nv) for k in range(1, nv)]
    edge = (0, rows - 1)

    local = [
        pltpu.make_async_copy(wind, own.at[v, :, pl.ds(0, 3)], own_sem.at[0]),
        pltpu.make_async_copy(depth, own.at[v, :, 3], own_sem.at[1]),
        pltpu.make_async_copy(x_hbm, ping, x_sem.at[0]),
    ]
    for copy in local:
        copy.start()

    barrier = pltpu.get_barrier_semaphore()
    for peer in peers:
        pl.semaphore_signal(barrier, inc=1, device_id={"vec": peer}, device_id_type=MESH)
    for side in range(2):
        @pl.when(has[side])
        def _(side=side):
            pl.semaphore_signal(barrier, inc=1, device_id={"lat": other[side]}, device_id_type=MESH)
        @pl.when(reaches[side])
        def _(side=side):
            pl.semaphore_signal(barrier, inc=1, device_id={"lat": far[side]}, device_id_type=MESH)
    pl.semaphore_wait(barrier, nv - 1 + sum(flag.astype(jnp.int32) for flag in has + reaches))

    def remote(src, dst, send, recv, target):
        return pltpu.make_async_remote_copy(
            src_ref=src, dst_ref=dst, send_sem=send, recv_sem=recv,
            device_id=target, device_id_type=MESH,
        )

    def lap(s):
        return lax.rem(s, 2)

    def source(side, s, k):
        return x_hbm.at[k, :, pl.ds(edge[side], 1), :] if s == 0 else leaving.at[side, s - 1, k]

    def direct(side, s, k):
        return remote(
            source(side, s, k), halo.at[side, s, k],
            hs.at[side], hr.at[side, lap(s), k], {"lat": other[side]})

    def detour(side, s, k):
        return remote(
            source(side, s, k), transit.at[s, k],
            hs.at[side], tr.at[lap(s), k], {"lat": other[1 - side]})

    def arrival(side, s, k):
        at = transit.at[s, k]
        return remote(at, at, hs.at[side], tr.at[lap(s), k], {"lat": other[1 - side]})

    def onward(side, s, k):
        return remote(
            transit.at[s, k], halo.at[side, s, k],
            ts.at[0], hr.at[side, lap(s), k], {"lat": far[side]})

    def send(s, k):
        for side in range(2):
            @pl.when(turn(relayed[side], s, k))
            def _(side=side):
                detour(side, s, k).start()
        for side in range(2):
            @pl.when(has[side] & jnp.logical_not(turn(relayed[side], s, k)))
            def _(side=side):
                direct(side, s, k).start()

    def relay(s, k, due=None):
        for side in range(2):
            @pl.when(turn(relaying[side], s, k) if due is None else due[side])
            def _(side=side):
                arrival(side, s, k).wait_recv()
                onward(side, s, k).start()

    def sent():
        for side in range(2):
            @pl.when(has[side])
            def _(side=side):
                whole = halo.at[side, pl.ds(0, steps)]
                remote(whole, whole, hs.at[side], hr.at[side, 0, 0], {"lat": other[side]}).wait_send()
            for number in range(1, count + 1):
                @pl.when(relaying[side] == number)
                def _(side=side, number=number):
                    whole = transit.at[:, pl.ds(0, number)]
                    remote(whole, whole, ts.at[0], tr.at[0, 0], {"lat": far[side]}).wait_send()

    def spread(s, n, peer):
        return [
            remote(wind.at[s], own.at[v, s, pl.ds(0, 3)], gs.at[n], gr.at[s], {"vec": peer}),
            remote(depth.at[s], own.at[v, s, 3], gs.at[n], gr.at[s], {"vec": peer}),
        ]

    def gathered(s):
        whole = own.at[pl.ds(0, nv - 1), s]
        return remote(whole, whole, gs.at[0], gr.at[s], {"vec": peers[0]})

    send(0, 0)
    for n, peer in enumerate(peers):
        for copy in spread(0, n, peer):
            copy.start()

    @pl.loop(1, count)
    def _(k):
        send(0, k)

    for s in range(1, steps):
        for n, peer in enumerate(peers):
            for copy in spread(s, n, peer):
                copy.start()

    for side in range(2):
        @pl.when(jnp.logical_not(has[side]))
        def _(side=side):
            halo[1 - side, steps, 0] = jnp.zeros((3, 1, width), jnp.float32)

    for k in range(LEAD):
        relay(0, k)
    for copy in local:
        copy.wait()

    def span(t):
        return pl.ds(t * LANES, LANES)

    for s in range(steps):
        gathered(s).wait_recv()
        for t in range(tiles):
            block, offset = divmod(t * LANES, part)
            a, b, d, c = (own[block, s, q, :, pl.ds(offset, LANES)] for q in range(4))
            a, b = half_step * a, half_step * b
            values = (side_weight - a, side_weight + a, side_weight - b, side_weight + b, time_step * d, half_step * c)
            for q, value in enumerate(values):
                table[q, :, span(t)] = value

        final = s == steps - 1
        old = (ping, pong)[s % 2]
        new = out if final else (ping, pong)[(s + 1) % 2]

        @pl.loop(0, count)
        def _(k, s=s, final=final, old=old, new=new):
            ahead = k + LEAD
            later = ahead >= count
            due = []
            for side in range(2):
                now = turn(relaying[side], s, ahead) & jnp.logical_not(later)
                if not final:
                    now |= turn(relaying[side], s + 1, ahead - count) & later
                due.append(now)
            relay(s + later.astype(jnp.int32), jnp.where(later, ahead - count, ahead), due)
            for side in range(2):
                @pl.when(has[1 - side])
                def _(side=side):
                    direct(side, s, k).wait_recv()
            slot = [
                (jnp.where(has[side], s, steps), jnp.where(has[side], k, 0)) for side in range(2)
            ]

            def load(f, t):
                return old[k, f, :, span(t)]

            def store(f, t, value):
                new[k, f, :, span(t)] = value
                if not final:
                    for side in range(2):
                        leaving[side, s, k, f, :, span(t)] = value[edge[side]:edge[side] + 1]

            def beyond(side, f, t):
                value = halo[1 - side, slot[side][0], slot[side][1], f, :, span(t)]
                return jnp.broadcast_to(value, (rows, LANES))

            def coefficient(q, t):
                return table[q, :, span(t)]

            sweep(load, store, beyond, coefficient, tiles)
            if not final:
                send(s + 1, k)

    for n, peer in enumerate(peers):
        remote(own.at[v], own.at[v], gs.at[n], gr.at[0], {"vec": peer}).wait_send()
    sent()


def solution(mesh):
    nv, nl = mesh.shape["vec"], mesh.shape["lat"]

    def shards(perturbation, wind_coriolis, depth_field):
        count, _, rows, width = perturbation.shape
        steps, part = wind_coriolis.shape[0], wind_coriolis.shape[3]
        dma = pltpu.SemaphoreType.DMA
        f32 = jnp.float32
        return pl.pallas_call(
            functools.partial(kernel, nv, nl),
            out_shape=jax.ShapeDtypeStruct(perturbation.shape, f32),
            in_specs=[pl.BlockSpec(memory_space=pltpu.HBM)] * 3,
            out_specs=pl.BlockSpec(memory_space=pltpu.VMEM),
            scratch_shapes=[
                pltpu.VMEM((count, 3, rows, width), f32),
                pltpu.VMEM((count, 3, rows, width), f32),
                pltpu.VMEM((2, steps - 1, count, 3, 1, width), f32),
                pltpu.VMEM((2, steps + 1, count, 3, 1, width), f32),
                pltpu.VMEM((steps, count, 3, 1, width), f32),
                pltpu.VMEM((nv, steps, 4, rows, part), f32),
                pltpu.VMEM((6, rows, width), f32),
                dma((1,)), dma((2,)),
                dma((nv - 1,)), dma((steps,)), dma((2,)), dma((2, 2, count)), dma((1,)), dma((2, count)),
            ],
            compiler_params=pltpu.CompilerParams(
                collective_id=0, has_side_effects=True, vmem_limit_bytes=40 * 1024 * 1024
            ),
        )(*(pltpu.with_memory_space_constraint(a, pltpu.HBM) for a in (perturbation, wind_coriolis, depth_field)))

    placed = (P("vec", None, "lat", None), P(None, None, "lat", "vec"), P(None, "lat", "vec"))
    return jax.shard_map(
        shards, mesh=mesh, in_specs=placed, out_specs=P("vec", None, "lat", None), check_vma=False
    )
```

time: 40 us -> 37.7 us (0.943)
  the two profiles are of different devices: /device:TPU:16 before, /device:TPU:0 now
where the time goes in v1:
time: 37.7 us; the launch traced here: 37.6 us
  Pallas kernels  36.4 us (97%)
  local copies, waits for them, and re-layouts  1.15 us (3%)
    pallas_call x1, Pallas kernels, shards(): pl.pallas_call(functools.partial(kernel, nv, nl), out_shape=jax.ShapeDtyp...  36.4 us
    unnamed x1, local copies, waits for them, and re-layouts  1.15 us

profile of v1, /device:TPU:0, one launch (start us, length us, event | category | flops | bytes accessed | tf_op | source)
XLA Modules:
  0.0 37.6 jit_solution(5264034018766450862)
XLA Ops:
  0.0 36.4 %shard_map.37 = f32[8,3,8,2048]{3,2,1,0:T(8,128)S(1)} custom-call(f32[8,3,8,2048]{3,2,1,0:T(8,128)} %x_hbm.1, f32[4,3,8,512]{3,2,1,0:T(8,128)} %wind.1, f32[4,8,512]{2,1,0:T(8,128)} %depth.1), custom_call_target="tpu_custom_call" | custom-call | tf_op jit(solution)/shard_map/pallas_call | solution.py:277
  36.4 1.1 %copy.5 = f32[8,3,8,2048]{3,2,1,0:T(8,128)} copy(f32[8,3,8,2048]{3,2,1,0:T(8,128)S(1)} %shard_map.37) | data formatting | bytes 3145728

commit v2 on v1

--- a/solution.py
+++ b/solution.py
@@ -84,17 +84,19 @@
     )
 
     def turn(number, s, k):
+        if s == 0:
+            return k >= count - number
         if s == steps - 1:
-            return k < number
+            return k < number // 2
         return lax.rem(k * (count - number), count) >= count - number
 
     peers = [lax.rem(v + k, nv) for k in range(1, nv)]
     edge = (0, rows - 1)
 
     local = [
+        pltpu.make_async_copy(x_hbm, ping, x_sem.at[0]),
         pltpu.make_async_copy(wind, own.at[v, :, pl.ds(0, 3)], own_sem.at[0]),
         pltpu.make_async_copy(depth, own.at[v, :, 3], own_sem.at[1]),
-        pltpu.make_async_copy(x_hbm, ping, x_sem.at[0]),
     ]
     for copy in local:
         copy.start()
@@ -121,26 +123,26 @@
         return lax.rem(s, 2)
 
     def source(side, s, k):
-        return x_hbm.at[k, :, pl.ds(edge[side], 1), :] if s == 0 else leaving.at[side, s - 1, k]
+        return ping.at[k, :, pl.ds(edge[side], 1), :] if s == 0 else leaving.at[side, s - 1, k]
 
     def direct(side, s, k):
         return remote(
             source(side, s, k), halo.at[side, s, k],
-            hs.at[side], hr.at[side, lap(s), k], {"lat": other[side]})
+            hs.at[side], hr.at[lap(s), k], {"lat": other[side]})
 
     def detour(side, s, k):
         return remote(
-            source(side, s, k), transit.at[s, k],
+            source(side, s, k), transit.at[s * count + k],
             hs.at[side], tr.at[lap(s), k], {"lat": other[1 - side]})
 
     def arrival(side, s, k):
-        at = transit.at[s, k]
+        at = transit.at[s * count + k]
         return remote(at, at, hs.at[side], tr.at[lap(s), k], {"lat": other[1 - side]})
 
     def onward(side, s, k):
         return remote(
-            transit.at[s, k], halo.at[side, s, k],
-            ts.at[0], hr.at[side, lap(s), k], {"lat": far[side]})
+            transit.at[s * count + k], halo.at[side, s, k],
+            ts.at[0], hr.at[lap(s), k], {"lat": far[side]})
 
     def send(s, k):
         for side in range(2):
@@ -164,11 +166,11 @@
             @pl.when(has[side])
             def _(side=side):
                 whole = halo.at[side, pl.ds(0, steps)]
-                remote(whole, whole, hs.at[side], hr.at[side, 0, 0], {"lat": other[side]}).wait_send()
+                remote(whole, whole, hs.at[side], hr.at[0, 0], {"lat": other[side]}).wait_send()
             for number in range(1, count + 1):
                 @pl.when(relaying[side] == number)
                 def _(side=side, number=number):
-                    whole = transit.at[:, pl.ds(0, number)]
+                    whole = transit.at[pl.ds(0, (steps - 1) * number + number // 2)]
                     remote(whole, whole, ts.at[0], tr.at[0, 0], {"lat": far[side]}).wait_send()
 
     def spread(s, n, peer):
@@ -181,6 +183,7 @@
         whole = own.at[pl.ds(0, nv - 1), s]
         return remote(whole, whole, gs.at[0], gr.at[s], {"vec": peers[0]})
 
+    local[0].wait()
     send(0, 0)
     for n, peer in enumerate(peers):
         for copy in spread(0, n, peer):
@@ -202,7 +205,7 @@
 
     for k in range(LEAD):
         relay(0, k)
-    for copy in local:
+    for copy in local[1:]:
         copy.wait()
 
     def span(t):
@@ -219,8 +222,8 @@
                 table[q, :, span(t)] = value
 
         final = s == steps - 1
-        old = (ping, pong)[s % 2]
-        new = out if final else (ping, pong)[(s + 1) % 2]
+        old = ping if s == 0 else (out, pong)[s % 2]
+        new = (pong, out)[s % 2]
 
         @pl.loop(0, count)
         def _(k, s=s, final=final, old=old, new=new):
@@ -233,10 +236,11 @@
                     now |= turn(relaying[side], s + 1, ahead - count) & later
                 due.append(now)
             relay(s + later.astype(jnp.int32), jnp.where(later, ahead - count, ahead), due)
-            for side in range(2):
-                @pl.when(has[1 - side])
-                def _(side=side):
-                    direct(side, s, k).wait_recv()
+            for ends in (1, 2):
+                @pl.when(has[0].astype(jnp.int32) + has[1].astype(jnp.int32) == ends)
+                def _(ends=ends):
+                    both = halo.at[pl.ds(0, ends), s, k]
+                    remote(both, both, hs.at[0], hr.at[lap(s), k], {"lat": other[0]}).wait_recv()
             slot = [
                 (jnp.where(has[side], s, steps), jnp.where(has[side], k, 0)) for side in range(2)
             ]
@@ -284,11 +288,11 @@
                 pltpu.VMEM((count, 3, rows, width), f32),
                 pltpu.VMEM((2, steps - 1, count, 3, 1, width), f32),
                 pltpu.VMEM((2, steps + 1, count, 3, 1, width), f32),
-                pltpu.VMEM((steps, count, 3, 1, width), f32),
+                pltpu.VMEM((steps * count, 3, 1, width), f32),
                 pltpu.VMEM((nv, steps, 4, rows, part), f32),
                 pltpu.VMEM((6, rows, width), f32),
                 dma((1,)), dma((2,)),
-                dma((nv - 1,)), dma((steps,)), dma((2,)), dma((2, 2, count)), dma((1,)), dma((2, count)),
+                dma((nv - 1,)), dma((steps,)), dma((2,)), dma((2, count)), dma((1,)), dma((2, count)),
             ],
             compiler_params=pltpu.CompilerParams(
                 collective_id=0, has_side_effects=True, vmem_limit_bytes=40 * 1024 * 1024

time: 37.7 us -> 36 us (0.955)
  the two profiles are of different devices: /device:TPU:0 before, /device:TPU:16 now
where the time goes in v2:
time: 36 us; the launch traced here: 35.7 us
  Pallas kernels  34.5 us (96%)
  local copies, waits for them, and re-layouts  1.15 us (3%)
    pallas_call x1, Pallas kernels, shards(): pl.pallas_call(functools.partial(kernel, nv, nl), out_shape=jax.ShapeDtyp...  34.5 us
    unnamed x1, local copies, waits for them, and re-layouts  1.15 us

profile of v2, /device:TPU:16, one launch (start us, length us, event | category | flops | bytes accessed | tf_op | source)
XLA Modules:
  0.0 35.7 jit_solution(5273001139493406702)
XLA Ops:
  0.0 34.5 %shard_map.37 = f32[8,3,8,2048]{3,2,1,0:T(8,128)S(1)} custom-call(f32[8,3,8,2048]{3,2,1,0:T(8,128)} %x_hbm.1, f32[4,3,8,512]{3,2,1,0:T(8,128)} %wind.1, f32[4,8,512]{2,1,0:T(8,128)} %depth.1), custom_call_target="tpu_custom_call" | custom-call | tf_op jit(solution)/shard_map/pallas_call | solution.py:281
  34.5 1.1 %copy.5 = f32[8,3,8,2048]{3,2,1,0:T(8,128)} copy(f32[8,3,8,2048]{3,2,1,0:T(8,128)S(1)} %shard_map.37) | data formatting | bytes 3145728

commit v3 on v2

--- a/solution.py
+++ b/solution.py
@@ -57,7 +57,7 @@
     nv, nl, x_hbm, wind, depth, out,
     ping, pong, leaving, halo, transit, own, table,
     x_sem, own_sem,
-    gs, gr, hs, hr, ts, tr,
+    gs, gr, hs, hr, ts, tr, below, beside, across,
 ):
     count, _, rows, width = x_hbm.shape
     steps, part = wind.shape[0], wind.shape[3]
@@ -98,20 +98,22 @@
         pltpu.make_async_copy(wind, own.at[v, :, pl.ds(0, 3)], own_sem.at[0]),
         pltpu.make_async_copy(depth, own.at[v, :, 3], own_sem.at[1]),
     ]
+    mate = l + 1 - 2 * odd
+
+    barrier = pltpu.get_barrier_semaphore()
+
+    def greet(semaphore, wanted, device):
+        @pl.when(wanted)
+        def _():
+            pl.semaphore_signal(semaphore, inc=1, device_id=device, device_id_type=MESH)
+
+    pl.semaphore_signal(barrier, inc=1, device_id={"lat": mate}, device_id_type=MESH)
+    greet(barrier, reaches[1], {"lat": far[1]})
+    for peer in peers:
+        greet(barrier, peer > v, {"vec": peer})
     for copy in local:
         copy.start()
-
-    barrier = pltpu.get_barrier_semaphore()
-    for peer in peers:
-        pl.semaphore_signal(barrier, inc=1, device_id={"vec": peer}, device_id_type=MESH)
-    for side in range(2):
-        @pl.when(has[side])
-        def _(side=side):
-            pl.semaphore_signal(barrier, inc=1, device_id={"lat": other[side]}, device_id_type=MESH)
-        @pl.when(reaches[side])
-        def _(side=side):
-            pl.semaphore_signal(barrier, inc=1, device_id={"lat": far[side]}, device_id_type=MESH)
-    pl.semaphore_wait(barrier, nv - 1 + sum(flag.astype(jnp.int32) for flag in has + reaches))
+    pl.semaphore_wait(barrier, 1 + v + reaches[0].astype(jnp.int32))
 
     def remote(src, dst, send, recv, target):
         return pltpu.make_async_remote_copy(
@@ -144,13 +146,23 @@
             transit.at[s * count + k], halo.at[side, s, k],
             ts.at[0], hr.at[lap(s), k], {"lat": far[side]})
 
-    def send(s, k):
+    def send(s, k, which=(True, True)):
         for side in range(2):
-            @pl.when(turn(relayed[side], s, k))
-            def _(side=side):
-                detour(side, s, k).start()
+            near = odd == 1 - side
+            around = turn(relayed[side], s, k)
+            if which[0]:
+                @pl.when(around)
+                def _(side=side):
+                    detour(side, s, k).start()
         for side in range(2):
-            @pl.when(has[side] & jnp.logical_not(turn(relayed[side], s, k)))
+            near = odd == 1 - side
+            around = turn(relayed[side], s, k)
+            straight = has[side] & jnp.logical_not(around)
+            if not which[0]:
+                straight &= jnp.logical_not(near)
+            if not which[1]:
+                straight &= near
+            @pl.when(straight)
             def _(side=side):
                 direct(side, s, k).start()
 
@@ -175,28 +187,56 @@
 
     def spread(s, n, peer):
         return [
-            remote(wind.at[s], own.at[v, s, pl.ds(0, 3)], gs.at[n], gr.at[s], {"vec": peer}),
-            remote(depth.at[s], own.at[v, s, 3], gs.at[n], gr.at[s], {"vec": peer}),
+            remote(wind.at[s], own.at[v, s, pl.ds(0, 3)], gs.at[0], gr.at[s], {"vec": peer}),
+            remote(depth.at[s], own.at[v, s, 3], gs.at[0], gr.at[s], {"vec": peer}),
         ]
 
     def gathered(s):
         whole = own.at[pl.ds(0, nv - 1), s]
         return remote(whole, whole, gs.at[0], gr.at[s], {"vec": peers[0]})
 
+    greet(below, reaches[0], {"lat": far[0]})
+    greet(beside, (odd == 1) & reaches[0], {"lat": mate})
+    for peer in peers:
+        greet(across, peer < v, {"vec": peer})
     local[0].wait()
-    send(0, 0)
-    for n, peer in enumerate(peers):
-        for copy in spread(0, n, peer):
-            copy.start()
-
-    @pl.loop(1, count)
+
+    @pl.loop(0, count)
     def _(k):
-        send(0, k)
-
+        send(0, k, (True, False))
+
+    def share_out(s, wanted):
+        for n, peer in enumerate(peers):
+            @pl.when(wanted(peer))
+            def _(s=s, n=n, peer=peer):
+                for copy in spread(s, n, peer):
+                    copy.start()
+
+    share_out(0, lambda peer: peer < v)
+
+    @pl.when((odd == 1) & reaches[1])
+    def _():
+        pl.semaphore_wait(below, 1)
+
+    @pl.when((odd == 0) & reaches[0])
+    def _():
+        pl.semaphore_wait(beside, 1)
+
+    @pl.loop(0, count)
+    def _(k):
+        send(0, k, (False, True))
+
+    @pl.when(v < nv - 1)
+    def _():
+        pl.semaphore_wait(across, nv - 1 - v)
+
+    share_out(0, lambda peer: peer > v)
     for s in range(1, steps):
-        for n, peer in enumerate(peers):
-            for copy in spread(s, n, peer):
-                copy.start()
+        share_out(s, lambda peer: peer >= 0)
+
+    @pl.when((odd == 0) & reaches[1])
+    def _():
+        pl.semaphore_wait(below, 1)
 
     for side in range(2):
         @pl.when(jnp.logical_not(has[side]))
@@ -222,8 +262,8 @@
                 table[q, :, span(t)] = value
 
         final = s == steps - 1
-        old = ping if s == 0 else (out, pong)[s % 2]
-        new = (pong, out)[s % 2]
+        old = ping if s == 0 else (out, pong)[(steps - s) % 2]
+        new = (out, pong)[(steps - 1 - s) % 2]
 
         @pl.loop(0, count)
         def _(k, s=s, final=final, old=old, new=new):
@@ -265,8 +305,8 @@
             if not final:
                 send(s + 1, k)
 
-    for n, peer in enumerate(peers):
-        remote(own.at[v], own.at[v], gs.at[n], gr.at[0], {"vec": peer}).wait_send()
+    whole = own.at[pl.ds(0, nv - 1)]
+    remote(whole, whole, gs.at[0], gr.at[0], {"vec": peers[0]}).wait_send()
     sent()
 
 
@@ -292,7 +332,8 @@
                 pltpu.VMEM((nv, steps, 4, rows, part), f32),
                 pltpu.VMEM((6, rows, width), f32),
                 dma((1,)), dma((2,)),
-                dma((nv - 1,)), dma((steps,)), dma((2,)), dma((2, count)), dma((1,)), dma((2, count)),
+                dma((1,)), dma((steps,)), dma((2,)), dma((2, count)), dma((1,)), dma((2, count)),
+                pltpu.SemaphoreType.REGULAR, pltpu.SemaphoreType.REGULAR, pltpu.SemaphoreType.REGULAR,
             ],
             compiler_params=pltpu.CompilerParams(
                 collective_id=0, has_side_effects=True, vmem_limit_bytes=40 * 1024 * 1024

time: 36 us -> 35.7 us (level)
  no operation moved by 1% of the time
where the time goes in v3:
time: 35.7 us; the launch traced here: 35.5 us
  Pallas kernels  34.4 us (96%)
  local copies, waits for them, and re-layouts  1.15 us (3%)
    pallas_call x1, Pallas kernels, shards(): pl.pallas_call(functools.partial(kernel, nv, nl), out_shape=jax.ShapeDtyp...  34.4 us
    unnamed x1, local copies, waits for them, and re-layouts  1.15 us

profile of v3, /device:TPU:16, one launch (start us, length us, event | category | flops | bytes accessed | tf_op | source)
XLA Modules:
  0.0 35.5 jit_solution(7200623327255208780)
XLA Ops:
  0.0 34.4 %shard_map.37 = f32[8,3,8,2048]{3,2,1,0:T(8,128)S(1)} custom-call(f32[8,3,8,2048]{3,2,1,0:T(8,128)} %x_hbm.1, f32[4,3,8,512]{3,2,1,0:T(8,128)} %wind.1, f32[4,8,512]{2,1,0:T(8,128)} %depth.1), custom_call_target="tpu_custom_call" | custom-call | tf_op jit(solution)/shard_map/pallas_call | solution.py:321
  34.4 1.1 %copy.5 = f32[8,3,8,2048]{3,2,1,0:T(8,128)} copy(f32[8,3,8,2048]{3,2,1,0:T(8,128)S(1)} %shard_map.37) | data formatting | bytes 3145728

commit v4 on v3

--- a/solution.py
+++ b/solution.py
@@ -125,7 +125,7 @@
         return lax.rem(s, 2)
 
     def source(side, s, k):
-        return ping.at[k, :, pl.ds(edge[side], 1), :] if s == 0 else leaving.at[side, s - 1, k]
+        return x_hbm.at[k, :, pl.ds(edge[side], 1), :] if s == 0 else leaving.at[side, s - 1, k]
 
     def direct(side, s, k):
         return remote(
@@ -199,8 +199,6 @@
     greet(beside, (odd == 1) & reaches[0], {"lat": mate})
     for peer in peers:
         greet(across, peer < v, {"vec": peer})
-    local[0].wait()
-
     @pl.loop(0, count)
     def _(k):
         send(0, k, (True, False))
@@ -245,7 +243,7 @@
 
     for k in range(LEAD):
         relay(0, k)
-    for copy in local[1:]:
+    for copy in local:
         copy.wait()
 
     def span(t):

time: 35.7 us -> 35.4 us (level)
  Pallas kernels: 34.4 us -> 33.7 us
    pallas_call x1, Pallas kernels: 34.4 us -> 33.7 us  [shards(): pl.pallas_call(functools.partial(kernel, nv, nl), out_shape=jax.ShapeDtyp...]
where the time goes in v4:
time: 35.4 us; the launch traced here: 34.9 us
  Pallas kernels  33.7 us (95%)
  local copies, waits for them, and re-layouts  1.15 us (3%)
    pallas_call x1, Pallas kernels, shards(): pl.pallas_call(functools.partial(kernel, nv, nl), out_shape=jax.ShapeDtyp...  33.7 us
    unnamed x1, local copies, waits for them, and re-layouts  1.15 us

profile of v4, /device:TPU:16, one launch (start us, length us, event | category | flops | bytes accessed | tf_op | source)
XLA Modules:
  0.0 34.9 jit_solution(11127962184022829899)
XLA Ops:
  0.0 33.7 %shard_map.37 = f32[8,3,8,2048]{3,2,1,0:T(8,128)S(1)} custom-call(f32[8,3,8,2048]{3,2,1,0:T(8,128)} %x_hbm.1, f32[4,3,8,512]{3,2,1,0:T(8,128)} %wind.1, f32[4,8,512]{2,1,0:T(8,128)} %depth.1), custom_call_target="tpu_custom_call" | custom-call | tf_op jit(solution)/shard_map/pallas_call | solution.py:319
  33.7 1.1 %copy.5 = f32[8,3,8,2048]{3,2,1,0:T(8,128)} copy(f32[8,3,8,2048]{3,2,1,0:T(8,128)S(1)} %shard_map.37) | data formatting | bytes 3145728

commit v5 on v4

--- a/solution.py
+++ b/solution.py
@@ -71,24 +71,32 @@
     odd = lax.rem(l, 2)
     place = l // 2
 
-    def share(number, wanted):
-        return jnp.where(wanted, number * count // pairs, 0) if nl % 2 == 0 else jnp.int32(0)
+    def rank(number, wanted):
+        return jnp.where(wanted, number, 0) if nl % 2 == 0 else jnp.int32(0)
 
     relayed = (
-        share(place, (odd == 0) & reaches[0]),
-        share(pairs - 1 - place, (odd == 1) & reaches[1]),
+        rank(place, (odd == 0) & reaches[0]),
+        rank(pairs - 1 - place, (odd == 1) & reaches[1]),
     )
     relaying = (
-        share(place, (odd == 1) & reaches[0]),
-        share(pairs - 1 - place, (odd == 0) & reaches[1]),
+        rank(place, (odd == 1) & reaches[0]),
+        rank(pairs - 1 - place, (odd == 0) & reaches[1]),
     )
 
+    def share(number, s):
+        if s == steps - 1:
+            return number * count // pairs // 2
+        if s == 1:
+            return number * (count - 1) // max(pairs - 1, 1)
+        return number * count // pairs
+
     def turn(number, s, k):
+        held = share(number, s)
         if s == 0:
-            return k >= count - number
+            return k >= count - held
         if s == steps - 1:
-            return k < number // 2
-        return lax.rem(k * (count - number), count) >= count - number
+            return k < held
+        return lax.rem(k * (count - held), count) >= count - held
 
     peers = [lax.rem(v + k, nv) for k in range(1, nv)]
     edge = (0, rows - 1)
@@ -111,8 +119,6 @@
     greet(barrier, reaches[1], {"lat": far[1]})
     for peer in peers:
         greet(barrier, peer > v, {"vec": peer})
-    for copy in local:
-        copy.start()
     pl.semaphore_wait(barrier, 1 + v + reaches[0].astype(jnp.int32))
 
     def remote(src, dst, send, recv, target):
@@ -179,10 +185,14 @@
             def _(side=side):
                 whole = halo.at[side, pl.ds(0, steps)]
                 remote(whole, whole, hs.at[side], hr.at[0, 0], {"lat": other[side]}).wait_send()
-            for number in range(1, count + 1):
+            for number in range(1, pairs):
+                total = sum(share(number, s) for s in range(steps))
+                if total == 0:
+                    continue
+
                 @pl.when(relaying[side] == number)
-                def _(side=side, number=number):
-                    whole = transit.at[pl.ds(0, (steps - 1) * number + number // 2)]
+                def _(side=side, total=total):
+                    whole = transit.at[pl.ds(0, total)]
                     remote(whole, whole, ts.at[0], tr.at[0, 0], {"lat": far[side]}).wait_send()
 
     def spread(s, n, peer):
@@ -194,12 +204,15 @@
     def gathered(s):
         whole = own.at[pl.ds(0, nv - 1), s]
         return remote(whole, whole, gs.at[0], gr.at[s], {"vec": peers[0]})
-
+    send(0, 0, (True, False))
+    for copy in local:
+        copy.start()
     greet(below, reaches[0], {"lat": far[0]})
     greet(beside, (odd == 1) & reaches[0], {"lat": mate})
     for peer in peers:
         greet(across, peer < v, {"vec": peer})
-    @pl.loop(0, count)
+
+    @pl.loop(1, count)
     def _(k):
         send(0, k, (True, False))
 

time: 35.4 us -> 35.2 us (level)
  no operation moved by 1% of the time
where the time goes in v5:
time: 35.2 us; the launch traced here: 34.9 us
  Pallas kernels  33.7 us (96%)
  local copies, waits for them, and re-layouts  1.15 us (3%)
    pallas_call x1, Pallas kernels, shards(): pl.pallas_call(functools.partial(kernel, nv, nl), out_shape=jax.ShapeDtyp...  33.7 us
    unnamed x1, local copies, waits for them, and re-layouts  1.15 us

profile of v5, /device:TPU:16, one launch (start us, length us, event | category | flops | bytes accessed | tf_op | source)
XLA Modules:
  0.0 34.9 jit_solution(1040721589185559467)
XLA Ops:
  0.0 33.7 %shard_map.37 = f32[8,3,8,2048]{3,2,1,0:T(8,128)S(1)} custom-call(f32[8,3,8,2048]{3,2,1,0:T(8,128)} %x_hbm.1, f32[4,3,8,512]{3,2,1,0:T(8,128)} %wind.1, f32[4,8,512]{2,1,0:T(8,128)} %depth.1), custom_call_target="tpu_custom_call" | custom-call | tf_op jit(solution)/shard_map/pallas_call | solution.py:332
  33.7 1.1 %copy.5 = f32[8,3,8,2048]{3,2,1,0:T(8,128)} copy(f32[8,3,8,2048]{3,2,1,0:T(8,128)S(1)} %shard_map.37) | data formatting | bytes 3145728

commit v6 on v5

--- a/solution.py
+++ b/solution.py
@@ -104,7 +104,7 @@
     local = [
         pltpu.make_async_copy(x_hbm, ping, x_sem.at[0]),
         pltpu.make_async_copy(wind, own.at[v, :, pl.ds(0, 3)], own_sem.at[0]),
-        pltpu.make_async_copy(depth, own.at[v, :, 3], own_sem.at[1]),
+        pltpu.make_async_copy(depth, own.at[v, :, 3], own_sem.at[0]),
     ]
     mate = l + 1 - 2 * odd
 
@@ -136,16 +136,16 @@
     def direct(side, s, k):
         return remote(
             source(side, s, k), halo.at[side, s, k],
-            hs.at[side], hr.at[lap(s), k], {"lat": other[side]})
+            hs.at[0], hr.at[lap(s), k], {"lat": other[side]})
 
     def detour(side, s, k):
         return remote(
             source(side, s, k), transit.at[s * count + k],
-            hs.at[side], tr.at[lap(s), k], {"lat": other[1 - side]})
+            hs.at[0], tr.at[lap(s), k], {"lat": other[1 - side]})
 
     def arrival(side, s, k):
         at = transit.at[s * count + k]
-        return remote(at, at, hs.at[side], tr.at[lap(s), k], {"lat": other[1 - side]})
+        return remote(at, at, hs.at[0], tr.at[lap(s), k], {"lat": other[1 - side]})
 
     def onward(side, s, k):
         return remote(
@@ -180,11 +180,12 @@
                 onward(side, s, k).start()
 
     def sent():
+        for ends in (1, 2):
+            @pl.when(has[0].astype(jnp.int32) + has[1].astype(jnp.int32) == ends)
+            def _(ends=ends):
+                whole = halo.at[pl.ds(0, ends), pl.ds(0, steps)]
+                remote(whole, whole, hs.at[0], hr.at[0, 0], {"lat": other[0]}).wait_send()
         for side in range(2):
-            @pl.when(has[side])
-            def _(side=side):
-                whole = halo.at[side, pl.ds(0, steps)]
-                remote(whole, whole, hs.at[side], hr.at[0, 0], {"lat": other[side]}).wait_send()
             for number in range(1, pairs):
                 total = sum(share(number, s) for s in range(steps))
                 if total == 0:
@@ -256,8 +257,8 @@
 
     for k in range(LEAD):
         relay(0, k)
-    for copy in local:
-        copy.wait()
+    local[0].wait()
+    pltpu.make_async_copy(own.at[v], own.at[v], own_sem.at[0]).wait()
 
     def span(t):
         return pl.ds(t * LANES, LANES)
@@ -342,8 +343,8 @@
                 pltpu.VMEM((steps * count, 3, 1, width), f32),
                 pltpu.VMEM((nv, steps, 4, rows, part), f32),
                 pltpu.VMEM((6, rows, width), f32),
-                dma((1,)), dma((2,)),
-                dma((1,)), dma((steps,)), dma((2,)), dma((2, count)), dma((1,)), dma((2, count)),
+                dma((1,)), dma((1,)),
+                dma((1,)), dma((steps,)), dma((1,)), dma((2, count)), dma((1,)), dma((2, count)),
                 pltpu.SemaphoreType.REGULAR, pltpu.SemaphoreType.REGULAR, pltpu.SemaphoreType.REGULAR,
             ],
             compiler_params=pltpu.CompilerParams(

time: 35.2 us -> 35.1 us (level)
  no operation moved by 1% of the time
where the time goes in v6:
time: 35.1 us; the launch traced here: 34.9 us
  Pallas kernels  33.7 us (96%)
  local copies, waits for them, and re-layouts  1.15 us (3%)
    pallas_call x1, Pallas kernels, shards(): pl.pallas_call(functools.partial(kernel, nv, nl), out_shape=jax.ShapeDtyp...  33.7 us
    unnamed x1, local copies, waits for them, and re-layouts  1.15 us

profile of v6, /device:TPU:16, one launch (start us, length us, event | category | flops | bytes accessed | tf_op | source)
XLA Modules:
  0.0 34.9 jit_solution(8222945838312152444)
XLA Ops:
  0.0 33.7 %shard_map.37 = f32[8,3,8,2048]{3,2,1,0:T(8,128)S(1)} custom-call(f32[8,3,8,2048]{3,2,1,0:T(8,128)} %x_hbm.1, f32[4,3,8,512]{3,2,1,0:T(8,128)} %wind.1, f32[4,8,512]{2,1,0:T(8,128)} %depth.1), custom_call_target="tpu_custom_call" | custom-call | tf_op jit(solution)/shard_map/pallas_call | solution.py:333
  33.7 1.1 %copy.5 = f32[8,3,8,2048]{3,2,1,0:T(8,128)} copy(f32[8,3,8,2048]{3,2,1,0:T(8,128)S(1)} %shard_map.37) | data formatting | bytes 3145728
